TPU v7x, 32 devices: a whole 2x2x4 slice. The times are simulated.
32 devices in a mesh: row: 4 (over z), col: 8 (over y, x, core).
Axes of the slice: x: 2, y: 2, z: 4, core: 2. Of those that a mesh axis runs over, the one named last changes fastest.
Arguments:
- amplitudes: bfloat16 [2048, 8192], P(('col', 'row')), may hold values from -6 to 6
- integrals: bfloat16 [8192, 8192], P('row', 'col'), may hold values from -0.0625 to 0.0625
- integral_tiles: int32 [64, 64], P('row', 'col'), may hold values from 0 to 1, as said below
- amplitude_tiles: int32 [16, 64], P('col'), may hold values 0 or 1
Outputs:
- ladder: float32 [2048, 8192], P('col', 'row')
Inputs may be any that keep to these rules, and one draw needn't show every extreme that they name: `integral_tiles`: tiles of higher ab index are more often nonzero.
All inputs are finite; a program needn't handle non-finite values. No bound on the sum of `amplitude_tiles` on one device may be relied on, other than what follows from the above.
Results may differ from a plain program's by a relative error of at most 0.0003.
Values may be sent and summed in bfloat16 or wider, within the bound.
No kernel may reach another device: no remote copies, remote signals or barrier semaphores. Data moves between devices by JAX's collectives and lax.ppermute only.
A program may use at most 128 MiB of HBM per device.

v0:
```python
import jax
import jax.numpy as jnp
from jax import lax
from jax.sharding import PartitionSpec as P

TILE = 128


def contract(left, right):
    return lax.dot_general(
        left, right, (((1,), (1,)), ((), ())), preferred_element_type=jnp.float32
    )


def on_device(amplitudes, integrals, integral_tiles, amplitude_tiles):
    local_rows = amplitudes.shape[0]
    tile_rows = jnp.repeat(amplitude_tiles, TILE, axis=0)
    tile_rows = lax.dynamic_slice_in_dim(
        tile_rows, lax.axis_index("row") * local_rows, local_rows, 0
    )
    amp_mask = jnp.repeat(tile_rows, TILE, axis=1).astype(jnp.bfloat16)
    masked_amps = amplitudes * amp_mask
    int_mask = jnp.repeat(jnp.repeat(integral_tiles, TILE, axis=0), TILE, axis=1).astype(
        jnp.bfloat16
    )
    masked_ints = integrals * int_mask
    panel = lax.all_gather(masked_amps, "row", axis=0, tiled=True)
    return contract(panel, lax.all_gather(masked_ints, "col", axis=1, tiled=True))


def solution(mesh):
    return jax.shard_map(
        on_device,
        mesh=mesh,
        in_specs=(P(("col", "row"), None), P("row", "col"), P("row", "col"), P("col", None)),
        out_specs=P("col", "row"),
        check_vma=False,
    )
```

profile of v0, /device:TPU:0, one launch (start us, length us, event | category | flops | bytes accessed | tf_op | source)
XLA Modules:
  0.0 279.3 jit_solution(6280737660417096425)
XLA Ops:
  6.5 0.0 copy-start.1
  6.5 0.0 all-gather.3.cloned.1.call-start
  6.5 0.7 broadcast_in_dim.12
  7.3 0.6 broadcast_in_dim.13
  7.9 2.8 %bitcast_multiply_fusion.1 = bf16[64,8192]{1,0:T(8,128)(2,1)} fusion(bf16[64,8192]{1,0:T(8,128)(2,1)} %param.4, bf16[8,8,64,128]{3,2,1,0:T(8,128)(2,1)S(1)} %bitcast.11), kind=kLoop, calls=%fused_computation.1 | loop fusion | flops 524288 | bytes 3145728 | tf_op jit(solution)/shard_map/mul | solution.py:22
  10.7 0.0 all-gather.3.cloned.1.call-update
  10.7 0.0 all-gather.5.cloned.1.call-start
  10.8 0.0 copy-done.1
  10.8 0.1 copy.5
  10.9 0.0 copy-start
  10.9 0.1 broadcast_in_dim.14
  11.0 5.8 %broadcast_in_dim.15 = bf16[2048,8,128]{2,1,0:T(8,128)(2,1)S(1)} broadcast(bf16[2048,8]{1,0:T(8,128)(2,1)S(1)} %bitcast.12), dimensions={0,1} | broadcast | bytes 4227072 | tf_op jit(solution)/shard_map/broadcast_in_dim | solution.py:23
  16.8 0.0 copy-done
  16.8 2.5 bitcast_multiply_fusion
  19.3 0.0 all-gather.5.cloned.1.call-update
  19.3 75.1 %all-gather.3.cloned.1.call-done = bf16[256,8192]{1,0:T(8,128)(2,1)} async-done(((bf16[64,8192]{1,0:T(8,128)(2,1)}), bf16[256,8192]{1,0:T(8,128)(2,1)}) %all-gather.3.cloned.1.call-update) | async-done | bytes 4194320 | tf_op jit(solution)/shard_map/all_gather | solution.py:27
  94.3 161.3 %all-gather.5.cloned.1.call-done = bf16[2048,8192]{1,0:T(8,128)(2,1)} async-done(((bf16[2048,1024]{1,0:T(8,128)(2,1)}), bf16[2048,8192]{1,0:T(8,128)(2,1)}) %all-gather.5.cloned.1.call-update) | async-done | bytes 33554448 | tf_op jit(solution)/shard_map/all_gather | solution.py:28
  255.6 16.9 %fusion = f32[256,2048]{1,0:T(8,128)} fusion(bf16[256,8192]{1,0:T(8,128)(2,1)} %all-gather.3.cloned.1.call-done, bf16[2048,8192]{1,0:T(8,128)(2,1)} %all-gather.5.cloned.1.call-done), kind=kOutput, calls=%fused_computation.3 | convolution fusion | flops 8589934592 | bytes 39845888 | tf_op jit(solution)/shard_map/dot_general | solution.py:10
  (2 shorter events, 0.0 us)
Async XLA Ops:
  6.5 4.2 %copy-start.1 = (s32[16,8]{0,1:T(8,128)S(1)}, s32[16,8]{0,1:T(8,128)}, u32[]{:S(2)}) copy-start(s32[16,8]{0,1:T(8,128)} %param.6) | copy-start | bytes 1540
  6.5 87.8 %all-gather.3.cloned.1.call-start = ((), (), s32[]{:S(2)}) async-start(), calls=%async_computation | async-start | bytes 5242880 | tf_op jit(solution)/shard_map/all_gather | solution.py:27
  10.7 244.9 %all-gather.5.cloned.1.call-start = ((), (), s32[]{:S(2)}) async-start(), calls=%async_computation.1 | async-start | bytes 37748736 | tf_op jit(solution)/shard_map/all_gather | solution.py:28
  10.9 5.9 %copy-start = (bf16[2048,1024]{1,0:T(8,128)(2,1)S(1)}, bf16[2048,1024]{1,0:T(8,128)(2,1)}, u32[]{:S(2)}) copy-start(bf16[2048,1024]{1,0:T(8,128)(2,1)} %param.5) | copy-start | bytes 12582916
Sparse Core Ops, SparseCore 0:
  10.8 83.4 all-gather.2
  96.2 159.3 all-gather.4
where the time goes:
time: 280 us; the launch traced here: 279 us
  waiting for transfers between devices  236 us (84%)
  matrix products  16.9 us (6%)
  between operations  13.5 us (5%)
  local copies, waits for them, and re-layouts  7.25 us (3%)
  other arithmetic  5.35 us (2%)
    all_gather x1, waiting for transfers between devices, on_device(): lax.all_gather(masked_ints, 'col', axis=1, tiled=True)  161 us
    all_gather x1, waiting for transfers between devices, on_device(): panel = lax.all_gather(masked_amps, 'row', axis=0, tiled=True)  75.1 us
    dot_general x1, matrix products, contract(): lax.dot_general(left, right, (((1,), (1,)), ((), ())), preferred_element_...  16.9 us
    broadcast_in_dim x1, local copies, waits for them, and re-layouts, on_device(): jnp.repeat(jnp.repeat(integral_tiles, TILE, axis=0), TILE, axis=1)  5.78 us
  transfers between devices with their start and end apart: 2, of which 2 were waited for; matrix products, arithmetic and copies ran while one was open for 3% of the time, Pallas kernels for 0%

commit v1 on v0

--- a/solution.py
+++ b/solution.py
@@ -1,9 +1,28 @@
+import functools
 import jax
 import jax.numpy as jnp
 from jax import lax
 from jax.sharding import PartitionSpec as P
+from jax.lax import axis_index, axis_size, ppermute
 
 TILE = 128
+
+
+def points_bring(frame_in, k_dim, chip_axis):
+    nodes = []
+    world = axis_size(chip_axis)
+    for b in range(world):
+        nodes.append((b, (b + 1) % world))
+    z1 = [None] * world
+    z1[world - 1] = frame_in
+    for hop_no in range(world - 2, -1, -1):
+        z1[hop_no] = ppermute(z1[hop_no + 1], chip_axis, nodes)
+    arr_out = jnp.concatenate(z1, axis=k_dim)
+    clean = (axis_index(chip_axis) + 1) * frame_in.shape[k_dim]
+    return jnp.roll(arr_out, clean, axis=k_dim)
+
+
+plan_loops = functools.partial(points_bring, k_dim=0, chip_axis="row")
 
 
 def contract(left, right):
@@ -24,7 +43,7 @@
         jnp.bfloat16
     )
     masked_ints = integrals * int_mask
-    panel = lax.all_gather(masked_amps, "row", axis=0, tiled=True)
+    panel = plan_loops(masked_amps)
     return contract(panel, lax.all_gather(masked_ints, "col", axis=1, tiled=True))
 
 

time: 280 us -> 206 us (0.74)
  waiting for transfers between devices: 236 us -> 148 us
  local copies, waits for them, and re-layouts: 7.25 us -> 17.5 us
  starting transfers between devices: 0.04 us -> 3.08 us
    all_gather x1, waiting for transfers between devices: 161 us -> 71.6 us  [on_device(): lax.all_gather(masked_ints, 'col', axis=1, tiled=True)]
    ppermute x0 -> x3, waiting for transfers between devices: none -> 76.6 us  [points_bring(): z1[hop_no] = ppermute(z1[hop_no + 1], chip_axis, nodes)]
    all_gather x1 -> x0, waiting for transfers between devices: 75.1 us -> none  [on_device(): panel = lax.all_gather(masked_amps, 'row', axis=0, tiled=True)]
    unnamed x4 -> x11, local copies, waits for them, and re-layouts: 0.01 us -> 9.86 us
    ppermute x0 -> x3, starting transfers between devices: none -> 3.08 us  [points_bring(): z1[hop_no] = ppermute(z1[hop_no + 1], chip_axis, nodes)]
  transfers between devices with their start and end apart: 2 -> 4, of which waited for: 2 -> 4; matrix products, arithmetic and copies ran while one was open for 3% -> 6% of each run, Pallas kernels for 0% -> 0%
where the time goes in v1:
time: 206 us; the launch traced here: 205 us
  waiting for transfers between devices  148 us (72%)
  local copies, waits for them, and re-layouts  17.5 us (8%)
  matrix products  16.9 us (8%)
  between operations  13.5 us (7%)
  other arithmetic  6.14 us (3%)
  starting transfers between devices  3.08 us (1%)
    ppermute x3, waiting for transfers between devices, points_bring(): z1[hop_no] = ppermute(z1[hop_no + 1], chip_axis, nodes)  76.6 us
    all_gather x1, waiting for transfers between devices, on_device(): lax.all_gather(masked_ints, 'col', axis=1, tiled=True)  71.6 us
    dot_general x1, matrix products, contract(): lax.dot_general(left, right, (((1,), (1,)), ((), ())), preferred_element_...  16.9 us
    unnamed x11, local copies, waits for them, and re-layouts  9.86 us
    broadcast_in_dim x1, local copies, waits for them, and re-layouts, on_device(): jnp.repeat(jnp.repeat(integral_tiles, TILE, axis=0), TILE, axis=1)  5.78 us
    mul x1, other arithmetic, on_device(): masked_ints = integrals * int_mask  4.75 us
  transfers between devices with their start and end apart: 4, of which 4 were waited for; matrix products, arithmetic and copies ran while one was open for 6% of the time, Pallas kernels for 0%

profile of v1, /device:TPU:0, one launch (start us, length us, event | category | flops | bytes accessed | tf_op | source)
XLA Modules:
  0.0 205.4 jit_solution(3931129885539760497)
XLA Ops:
  6.5 0.0 all-gather.2.cloned.1.call-start
  6.5 0.7 convert_element_type.20
  7.2 0.1 copy.5
  7.3 0.1 broadcast_in_dim.14
  7.4 5.8 %broadcast_in_dim.15 = bf16[2048,8,128]{2,1,0:T(8,128)(2,1)S(1)} broadcast(bf16[2048,8]{1,0:T(8,128)(2,1)S(1)} %bitcast.11), dimensions={0,1} | broadcast | bytes 4227072 | tf_op jit(solution)/shard_map/broadcast_in_dim | solution.py:42
  13.2 0.0 copy-start.1
  13.2 0.0 copy-start
  13.2 4.8 %bitcast_multiply_fusion = bf16[2048,1024]{1,0:T(8,128)(2,1)} fusion(bf16[2048,1024]{1,0:T(8,128)(2,1)} %param.5, bf16[256,8,8,128]{3,2,1,0:T(8,128)(2,1)S(1)} %bitcast.9), kind=kLoop, calls=%fused_computation | loop fusion | flops 2097152 | bytes 12582912 | tf_op jit(solution)/shard_map/mul | solution.py:45
  18.0 0.0 all-gather.2.cloned.1.call-update
  18.0 0.0 copy-done.1
  18.0 0.6 broadcast_in_dim.13
  18.6 0.0 copy-done
  18.7 0.7 bitcast_multiply_fusion.1
  19.4 3.1 %collective-permute-start = (bf16[64,8192]{1,0:T(8,128)(2,1)S(1)}, bf16[64,8192]{1,0:T(8,128)(2,1)S(1)}, u32[]{:S(2)}, u32[]{:S(2)}) collective-permute-start(bf16[64,8192]{1,0:T(8,128)(2,1)S(1)} %bitcast_multiply_fusion.1), channel_id=1, source_target_pairs={{0,8},{8,16},{16,24},{24,0},{1,9},{9,17},{17,25},{25,1},{2,10},{10... | collective-permute-start | bytes 3145736 | tf_op jit(solution)/shard_map/ppermute | solution.py:19
  22.4 25.2 %collective-permute-done = bf16[64,8192]{1,0:T(8,128)(2,1)S(1)} collective-permute-done((bf16[64,8192]{1,0:T(8,128)(2,1)S(1)}, bf16[64,8192]{1,0:T(8,128)(2,1)S(1)}, u32[]{:S(2)}, u32[]{:S(2)}) %collective-permute-start) | collective-permute-done | bytes 1048608 | tf_op jit(solution)/shard_map/ppermute | solution.py:19
  47.6 0.0 collective-permute-start.1
  47.6 26.1 %collective-permute-done.1 = bf16[64,8192]{1,0:T(8,128)(2,1)S(1)} collective-permute-done((bf16[64,8192]{1,0:T(8,128)(2,1)S(1)}, bf16[64,8192]{1,0:T(8,128)(2,1)S(1)}, u32[]{:S(2)}, u32[]{:S(2)}) %collective-permute-start.1) | collective-permute-done | bytes 1048608 | tf_op jit(solution)/shard_map/ppermute | solution.py:19
  73.8 0.0 collective-permute-start.2
  73.8 25.3 %collective-permute-done.2 = bf16[64,8192]{1,0:T(8,128)(2,1)} collective-permute-done((bf16[64,8192]{1,0:T(8,128)(2,1)S(1)}, bf16[64,8192]{1,0:T(8,128)(2,1)}, u32[]{:S(2)}, u32[]{:S(2)}) %collective-permute-start.2) | collective-permute-done | bytes 1048608 | tf_op jit(solution)/shard_map/ppermute | solution.py:19
  99.1 2.3 %constant_dynamic-update-slice_fusion.7 = bf16[512,8192]{1,0:T(8,128)(2,1)} fusion(bf16[64,8192]{1,0:T(8,128)(2,1)} %collective-permute-done.2), kind=kLoop, calls=%fused_computation.12 | loop fusion | bytes 2097152
  101.4 1.1 constant_dynamic-update-slice_fusion.6
  102.4 1.0 constant_dynamic-update-slice_fusion.5
  103.5 1.1 constant_dynamic-update-slice_fusion.4
  104.6 2.3 %constant_dynamic-update-slice_fusion.3 = bf16[512,8192]{1,0:T(8,128)(2,1)} fusion(bf16[512,8192]{1,0:T(8,128)(2,1)} %constant_dynamic-update-slice_fusion.4, bf16[64,8192]{1,0:T(8,128)(2,1)} %collective-permute-done.2), kind=kLoop, calls=%fused_computation.8 | loop fusion | bytes 2097152
  106.8 1.0 constant_dynamic-update-slice_fusion.2
  107.9 1.1 constant_dynamic-update-slice_fusion.1
  108.9 1.1 constant_dynamic-update-slice_fusion
  110.0 71.6 %all-gather.2.cloned.1.call-done = bf16[2048,8192]{1,0:T(8,128)(2,1)} async-done(((bf16[2048,1024]{1,0:T(8,128)(2,1)}), bf16[2048,8192]{1,0:T(8,128)(2,1)}) %all-gather.2.cloned.1.call-update) | async-done | bytes 33554448 | tf_op jit(solution)/shard_map/all_gather | solution.py:47
  181.6 16.9 %fusion = f32[256,2048]{1,0:T(8,128)} fusion(bf16[2048,8192]{1,0:T(8,128)(2,1)} %all-gather.2.cloned.1.call-done, bf16[512,8192]{1,0:T(8,128)(2,1)} %constant_dynamic-update-slice_fusion, s32[]{:T(128)S(6)} %select_n.18), kind=kOutput, calls=%fused_computation.1 | convolution fusion | flops 8589934592 | bytes 39845892 | tf_op jit(solution)/shard_map/dot_general | solution.py:29
  (2 shorter events, 0.0 us)
Async XLA Ops:
  6.5 175.1 %all-gather.2.cloned.1.call-start = ((), (), s32[]{:S(2)}) async-start(), calls=%async_computation | async-start | bytes 37748736 | tf_op jit(solution)/shard_map/all_gather | solution.py:47
  13.2 4.8 %copy-start.1 = (s32[2,64]{1,0:T(2,128)S(1)}, s32[2,64]{1,0:T(2,128)}, u32[]{:S(2)}) copy-start(s32[2,64]{1,0:T(2,128)} %param.7) | copy-start | bytes 1540
  13.2 5.5 %copy-start = (bf16[64,8192]{1,0:T(8,128)(2,1)S(1)}, bf16[64,8192]{1,0:T(8,128)(2,1)}, u32[]{:S(2)}) copy-start(bf16[64,8192]{1,0:T(8,128)(2,1)} %param.4) | copy-start | bytes 3145732
  19.4 28.3 %collective-permute-start = (bf16[64,8192]{1,0:T(8,128)(2,1)S(1)}, bf16[64,8192]{1,0:T(8,128)(2,1)S(1)}, u32[]{:S(2)}, u32[]{:S(2)}) collective-permute-start(bf16[64,8192]{1,0:T(8,128)(2,1)S(1)} %bitcast_multiply_fusion.1), channel_id=1, source_target_pairs={{0,8},{8,16},{16,24},{24,0},{1,9},{9,17},{17,25},{25,1},{2,10},{10... | collective-permute-start | bytes 3145736 | tf_op jit(solution)/shard_map/ppermute | solution.py:19
  47.6 26.1 %collective-permute-start.1 = (bf16[64,8192]{1,0:T(8,128)(2,1)S(1)}, bf16[64,8192]{1,0:T(8,128)(2,1)S(1)}, u32[]{:S(2)}, u32[]{:S(2)}) collective-permute-start(bf16[64,8192]{1,0:T(8,128)(2,1)S(1)} %collective-permute-done), channel_id=1, source_target_pairs={{0,8},{8,16},{16,24},{24,0},{1,9},{9,17},{17,25},{25,1},{2,10},{10... | collective-permute-start | bytes 3145736 | tf_op jit(solution)/shard_map/ppermute | solution.py:19
  73.8 25.3 %collective-permute-start.2 = (bf16[64,8192]{1,0:T(8,128)(2,1)S(1)}, bf16[64,8192]{1,0:T(8,128)(2,1)}, u32[]{:S(2)}, u32[]{:S(2)}) collective-permute-start(bf16[64,8192]{1,0:T(8,128)(2,1)S(1)} %collective-permute-done.1), channel_id=1, source_target_pairs={{0,8},{8,16},{16,24},{24,0},{1,9},{9,17},{17,25},{25,1},{2,10},{10... | collective-permute-start | bytes 3145736 | tf_op jit(solution)/shard_map/ppermute | solution.py:19
Sparse Core Ops, SparseCore 0:
  18.1 163.4 all-gather.1
